TPU v7x, 512 devices: a whole 4x8x8 slice. The times are simulated.
512 devices in a mesh: dp: 32 (over z, x), rows: 16 (over y, core).
Axes of the slice: x: 4, y: 8, z: 8, core: 2. Of those that a mesh axis runs over, the one named last changes fastest.
Arguments:
- older_output: bfloat16 [7680, 12, 2048], P(('dp', 'rows')), parts along dimension 0, may hold values from -6 to 6
- newer_output: bfloat16 [7680, 12, 2048], P(('dp', 'rows')), parts along dimension 0, may hold values from -6 to 6
- output_grad: bfloat16 [7680, 12, 2048], P(('dp', 'rows')), parts along dimension 0, may hold values from -6 to 6
- older_weight: bfloat16 [2048, 512], P('rows'), may hold values from -0.1875 to 0.1875
- newer_weight: bfloat16 [2048, 512], P('rows'), may hold values from -0.1875 to 0.1875
- square_point: bfloat16 [512, 512], P('rows'), may hold values from -0.25 to 0.25
- column_point: bfloat16 [512, 512], P('rows'), may hold values from -0.25 to 0.25
- square_kernel: float32 [3, 3, 512], replicated, may hold values from -2.4 to 2.4
- column_kernel: float32 [7, 512], replicated, may hold values from -2.4 to 2.4
Outputs:
- cell_output: bfloat16 [7680, 12, 2048], P(('dp', 'rows')), parts along dimension 0
- older_grad: bfloat16 [7680, 12, 2048], P(('dp', 'rows')), parts along dimension 0
- newer_grad: bfloat16 [7680, 12, 2048], P(('dp', 'rows')), parts along dimension 0
There are 32 independent parts, one for each index of `dp`. A program takes and returns all parts, laid end to end along the dimension named above; an argument that names none is the same for every part. Nothing has to cross between parts.
All inputs are finite; a program needn't handle non-finite values.
Results may differ from a plain program's by a relative error of at most 0.0057.
Values may be sent and summed in bfloat16 or wider, within the bound.
No kernel may reach another device: no remote copies, remote signals or barrier semaphores. Data moves between devices by JAX's collectives and lax.ppermute only.
A program may use at most 64 MiB of HBM per device.

v0:
```python
import jax
import jax.numpy as jnp
from jax import lax
from jax.sharding import PartitionSpec as P

HEIGHT = 30


def with_halo(block, sides, width):
    for axis, dim in sides:
        count = lax.axis_size(axis)
        forward = [(i, i + 1) for i in range(count - 1)]
        backward = [(target, source) for source, target in forward]
        low = lax.ppermute(
            lax.slice_in_dim(block, block.shape[dim] - width, None, axis=dim), axis, forward
        )
        high = lax.ppermute(lax.slice_in_dim(block, 0, width, axis=dim), axis, backward)
        block = jnp.concatenate([low, block, high], axis=dim)
    return block


def same_image(first_row, local_rows, offset):
    row_ids = jnp.arange(local_rows, dtype=jnp.int32) + first_row
    inside = jnp.floor_divide(row_ids + offset, HEIGHT) == jnp.floor_divide(row_ids, HEIGHT)
    return jnp.where(inside, 1.0, 0.0).astype(jnp.float32)[:, None, None]


def square_taps(padded, kernel, flip, first_row):
    full = jnp.pad(padded, ((0, 0), (1, 1), (0, 0))).astype(jnp.float32)
    height = full.shape[0] - 2
    across = full.shape[1] - 2
    total = jnp.zeros((height, across, full.shape[2]), jnp.float32)
    for i in range(3):
        keep = same_image(first_row, height, (2 - i if flip else i) - 1)
        for j in range(3):
            first = 2 - i if flip else i
            second = 2 - j if flip else j
            total = total + full[first : first + height, second : second + across, :] * (
                kernel[i, j] * keep
            )
    return total


def column_taps(padded, kernel, flip, first_row):
    full = padded.astype(jnp.float32)
    height = full.shape[0] - 6
    total = jnp.zeros((height, full.shape[1], full.shape[2]), jnp.float32)
    for i in range(7):
        first = 6 - i if flip else i
        keep = same_image(first_row, height, first - 3)
        total = total + full[first : first + height, :, :] * (kernel[i] * keep)
    return total


def local(
    older_output,
    newer_output,
    output_grad,
    older_weight,
    newer_weight,
    square_point,
    column_point,
    square_kernel,
    column_kernel,
):
    height, across, channels = older_output.shape
    filters = square_point.shape[1]
    shape_three = (height, across, filters)
    first_row = lax.axis_index("rows") * height
    pool_kernel = jnp.full((3, 3, filters), 1.0 / 9.0, jnp.float32)
    older_flat = older_output.reshape(-1, channels)
    newer_flat = newer_output.reshape(-1, channels)
    older_relu = jnp.maximum(older_flat, 0)
    newer_relu = jnp.maximum(newer_flat, 0)
    older_full, newer_full = (
        lax.all_gather(older_weight, "rows", axis=0, tiled=True),
        lax.all_gather(newer_weight, "rows", axis=0, tiled=True),
    )
    older_sum = jnp.dot(older_relu, older_full, preferred_element_type=jnp.float32)
    newer_sum = jnp.dot(newer_relu, newer_full, preferred_element_type=jnp.float32)
    older_mixed = older_sum.astype(jnp.bfloat16).reshape(shape_three)
    newer_mixed = newer_sum.astype(jnp.bfloat16).reshape(shape_three)
    square_full, column_full = (
        lax.all_gather(square_point, "rows", axis=0, tiled=True),
        lax.all_gather(column_point, "rows", axis=0, tiled=True),
    )
    older_rim = with_halo(older_mixed, (("rows", 0),), 3)
    newer_rim = with_halo(newer_mixed, (("rows", 0),), 1)
    square_pre = (
        square_taps(newer_rim, square_kernel, False, first_row)
        .astype(jnp.bfloat16)
        .reshape(-1, filters)
    )
    column_pre = (
        column_taps(older_rim, column_kernel, False, first_row)
        .astype(jnp.bfloat16)
        .reshape(-1, filters)
    )
    pooled = square_taps(older_rim[2:-2], pool_kernel, False, first_row).reshape(-1, filters)
    square_branch = jnp.dot(square_pre, square_full, preferred_element_type=jnp.float32)
    column_branch = jnp.dot(column_pre, column_full, preferred_element_type=jnp.float32)
    cell_output = jnp.concatenate(
        [
            square_branch,
            column_branch,
            pooled,
            newer_mixed.reshape(-1, filters).astype(jnp.float32),
        ],
        axis=1,
    )
    cell_output = cell_output.astype(jnp.bfloat16).reshape(height, across, 4 * filters)
    grads = output_grad.reshape(-1, 4 * filters)
    grad_square = grads[:, :filters]
    grad_column = grads[:, filters : 2 * filters]
    grad_pool = grads[:, 2 * filters : 3 * filters].reshape(shape_three)
    grad_same = grads[:, 3 * filters :].reshape(shape_three)
    square_back = (
        jnp.dot(grad_square, square_full.T, preferred_element_type=jnp.float32)
        .astype(jnp.bfloat16)
        .reshape(shape_three)
    )
    column_back = (
        jnp.dot(grad_column, column_full.T, preferred_element_type=jnp.float32)
        .astype(jnp.bfloat16)
        .reshape(shape_three)
    )
    column_rim = with_halo(column_back, (("rows", 0),), 3)
    square_rim, pool_rim = (
        with_halo(square_back, (("rows", 0),), 1),
        with_halo(grad_pool, (("rows", 0),), 1),
    )
    newer_back = (
        (square_taps(square_rim, square_kernel, True, first_row) + grad_same.astype(jnp.float32))
        .astype(jnp.bfloat16)
        .reshape(-1, filters)
    )
    older_back = (
        (
            column_taps(column_rim, column_kernel, True, first_row)
            + square_taps(pool_rim, pool_kernel, True, first_row)
        )
        .astype(jnp.bfloat16)
        .reshape(-1, filters)
    )
    older_mask = jnp.where(older_flat > 0, 1.0, 0.0).astype(jnp.float32)
    newer_mask = jnp.where(newer_flat > 0, 1.0, 0.0).astype(jnp.float32)
    older_term = jnp.dot(older_back, older_full.T, preferred_element_type=jnp.float32)
    newer_term = jnp.dot(newer_back, newer_full.T, preferred_element_type=jnp.float32)
    older_grad = (older_term * older_mask).astype(jnp.bfloat16).reshape(older_output.shape)
    newer_grad = (newer_term * newer_mask).astype(jnp.bfloat16).reshape(newer_output.shape)
    return (cell_output, older_grad, newer_grad)


def solution(mesh):
    in_specs = (
        P(("dp", "rows"), None, None),
        P(("dp", "rows"), None, None),
        P(("dp", "rows"), None, None),
        P("rows", None),
        P("rows", None),
        P("rows", None),
        P("rows", None),
        P(),
        P(),
    )
    out_specs = (
        P(("dp", "rows"), None, None),
        P(("dp", "rows"), None, None),
        P(("dp", "rows"), None, None),
    )
    return jax.shard_map(local, mesh=mesh, in_specs=in_specs, out_specs=out_specs, check_vma=False)
```

profile of v0, /device:TPU:1, one launch (start us, length us, event | category | flops | bytes accessed | tf_op | source)
XLA Modules:
  0.0 140.9 jit_solution(8323920743990531332)
XLA Ops:
  8.0 1.6 %copy.52 = bf16[15,12,2048]{2,1,0:T(8,128)(2,1)S(1)} copy(bf16[15,12,2048]{2,0,1:T(8,128)(2,1)} %param.11) | data formatting | bytes 1474560 | tf_op args[2]
  9.7 22.4 %all_gather.13 = bf16[512,512]{1,0:T(8,128)(2,1)S(1)} all-gather(bf16[32,512]{1,0:T(8,128)(2,1)S(1)} %copy-done.40), channel_id=1, replica_groups=mesh['dp'=32,'rows'=16] {'rows'}, dimensions={0}, use_global_device_ids=true | all-gather | bytes 557056 | tf_op jit(solution)/shard_map/all_gather | solution.py:84
  34.0 3.7 %collective-permute-start.8 = (bf16[1,12,512]{2,1,0:T(8,128)(2,1)}, bf16[1,12,512]{2,1,0:T(8,128)(2,1)}, u32[]{:S(2)}, u32[]{:S(2)}) collective-permute-start(bf16[1,12,512]{2,1,0:T(8,128)(2,1)} %get-tuple-element.18), channel_id=1, source_target_pairs={{0,1},{1,2},{2,3},{3,4},{4,5},{5,6},{6,7},{7,8},{8,9},{9,10},{10,1... | collective-permute-start | bytes 36872 | tf_op jit(solution)/shard_map/ppermute | solution.py:14
  37.7 1.9 %collective-permute-start.9 = (bf16[1,12,512]{2,1,0:T(8,128)(2,1)}, bf16[1,12,512]{2,1,0:T(8,128)(2,1)}, u32[]{:S(2)}, u32[]{:S(2)}) collective-permute-start(bf16[1,12,512]{2,1,0:T(8,128)(2,1)} %get-tuple-element.19), channel_id=1, source_target_pairs={{1,0},{2,1},{3,2},{4,3},{5,4},{6,5},{7,6},{8,7},{9,8},{10,9},{11,1... | collective-permute-start | bytes 36872 | tf_op jit(solution)/shard_map/ppermute | solution.py:17
  40.3 1.9 %collective-permute-start.7 = (bf16[1,12,512]{2,0,1:T(2,128)(2,1)}, bf16[1,12,512]{2,0,1:T(2,128)(2,1)}, u32[]{:S(2)}, u32[]{:S(2)}) collective-permute-start(bf16[1,12,512]{2,0,1:T(2,128)(2,1)} %copy.57), channel_id=1, source_target_pairs={{1,0},{2,1},{3,2},{4,3},{5,4},{6,5},{7,6},{8,7},{9,8},{10,9},{11,1... | collective-permute-start | bytes 36872 | tf_op jit(solution)/shard_map/ppermute | solution.py:17
  42.8 3.6 %collective-permute-start.6 = (bf16[1,12,512]{2,0,1:T(2,128)(2,1)}, bf16[1,12,512]{2,0,1:T(2,128)(2,1)}, u32[]{:S(2)}, u32[]{:S(2)}) collective-permute-start(bf16[1,12,512]{2,0,1:T(2,128)(2,1)} %copy.56), channel_id=1, source_target_pairs={{0,1},{1,2},{2,3},{3,4},{4,5},{5,6},{6,7},{7,8},{8,9},{9,10},{10,1... | collective-permute-start | bytes 36872 | tf_op jit(solution)/shard_map/ppermute | solution.py:14
  46.4 17.1 %all_gather.15 = bf16[512,512]{1,0:T(8,128)(2,1)S(1)} all-gather(bf16[32,512]{1,0:T(8,128)(2,1)S(1)} %copy-done.41), channel_id=1, replica_groups=mesh['dp'=32,'rows'=16] {'rows'}, dimensions={0}, use_global_device_ids=true | all-gather | bytes 557056 | tf_op jit(solution)/shard_map/all_gather | solution.py:85
  65.9 2.1 %collective-permute-start.5 = (bf16[3,12,512]{2,0,1:T(4,128)(2,1)}, bf16[3,12,512]{2,0,1:T(4,128)(2,1)}, u32[]{:S(2)}, u32[]{:S(2)}) collective-permute-start(bf16[3,12,512]{2,0,1:T(4,128)(2,1)} %copy.54), channel_id=1, source_target_pairs={{1,0},{2,1},{3,2},{4,3},{5,4},{6,5},{7,6},{8,7},{9,8},{10,9},{11,1... | collective-permute-start | bytes 110600 | tf_op jit(solution)/shard_map/ppermute | solution.py:17
  72.4 1.3 compare_select_fusion.1
  76.1 1.6 %copy.47 = bf16[15,12,2048]{2,1,0:T(8,128)(2,1)S(1)} copy(bf16[15,12,2048]{2,0,1:T(8,128)(2,1)} %broadcast_maximum_fusion) | data formatting | bytes 1474560 | tf_op jit(solution)/shard_map/max | solution.py:73
  83.4 2.3 %copy.60 = f32[15,12,2048]{2,1,0:T(8,128)S(1)} copy(f32[15,12,2048]{2,0,1:T(8,128)} %compare_select_fusion.1) | data formatting | bytes 2949120 | tf_op jit(solution)/shard_map/jit(_where)/select_n | solution.py:145
  85.7 1.4 select_n.201
  88.0 1.3 select_n.203
  89.3 3.5 %collective-permute-start.4 = (bf16[3,12,512]{2,0,1:T(4,128)(2,1)S(1)}, bf16[3,12,512]{2,0,1:T(4,128)(2,1)S(1)}, u32[]{:S(2)}, u32[]{:S(2)}) collective-permute-start(bf16[3,12,512]{2,0,1:T(4,128)(2,1)S(1)} %copy-done.39), channel_id=1, source_target_pairs={{0,1},{1,2},{2,3},{3,4},{4,5},{5,6},{6,7},{7,8},{8,9},{9,10},{10,1... | collective-permute-start | bytes 110600 | tf_op jit(solution)/shard_map/ppermute | solution.py:14
  98.1 2.2 %convolution_convert_fusion.4 = bf16[180,512]{1,0:T(8,128)(2,1)S(1)} fusion(bf16[180,2048]{1,0:T(8,128)(2,1)S(1)} %copy-done.8, bf16[2048,512]{1,0:T(8,128)(2,1)} %all-gather.5.cloned.1.call-done), kind=kOutput, calls=%fused_computation.10 | convolution fusion | flops 377579520 | bytes 3018752 | tf_op jit(solution)/shard_map/dot_general | solution.py:79
  100.5 2.1 %collective-permute-start.3 = (bf16[3,12,512]{2,0,1:T(4,128)(2,1)S(1)}, bf16[3,12,512]{2,0,1:T(4,128)(2,1)S(1)}, u32[]{:S(2)}, u32[]{:S(2)}) collective-permute-start(bf16[3,12,512]{2,0,1:T(4,128)(2,1)S(1)} %copy.49), channel_id=1, source_target_pairs={{1,0},{2,1},{3,2},{4,3},{5,4},{6,5},{7,6},{8,7},{9,8},{10,9},{11,1... | collective-permute-start | bytes 110600 | tf_op jit(solution)/shard_map/ppermute | solution.py:17
  102.5 7.8 %all-gather.3.cloned.1.call-done = bf16[2048,512]{1,0:T(8,128)(2,1)} async-done(((bf16[128,512]{1,0:T(8,128)(2,1)}), bf16[2048,512]{1,0:T(8,128)(2,1)}) %all-gather.3.cloned.1.call-update) | async-done | bytes 2097168 | tf_op jit(solution)/shard_map/all_gather | solution.py:77
  110.3 2.1 %convolution_convert_fusion.5 = bf16[180,512]{1,0:T(8,128)(2,1)S(1)} fusion(bf16[180,2048]{1,0:T(8,128)(2,1)S(1)} %copy-done.7, bf16[2048,512]{1,0:T(8,128)(2,1)} %all-gather.3.cloned.1.call-done), kind=kOutput, calls=%fused_computation.11 | convolution fusion | flops 377579520 | bytes 3018752 | tf_op jit(solution)/shard_map/dot_general | solution.py:80
  113.1 2.9 %collective-permute-start = (bf16[1,12,512]{2,1,0:T(8,128)(2,1)}, bf16[1,12,512]{2,1,0:T(8,128)(2,1)}, u32[]{:S(2)}, u32[]{:S(2)}) collective-permute-start(bf16[1,12,512]{2,1,0:T(8,128)(2,1)} %get-tuple-element.22), channel_id=1, source_target_pairs={{0,1},{1,2},{2,3},{3,4},{4,5},{5,6},{6,7},{7,8},{8,9},{9,10},{10,1... | collective-permute-start | bytes 36872 | tf_op jit(solution)/shard_map/ppermute | solution.py:14
  116.0 2.2 %collective-permute-start.1 = (bf16[1,12,512]{2,1,0:T(8,128)(2,1)}, bf16[1,12,512]{2,1,0:T(8,128)(2,1)}, u32[]{:S(2)}, u32[]{:S(2)}) collective-permute-start(bf16[1,12,512]{2,1,0:T(8,128)(2,1)} %get-tuple-element.23), channel_id=1, source_target_pairs={{1,0},{2,1},{3,2},{4,3},{5,4},{6,5},{7,6},{8,7},{9,8},{10,9},{11,1... | collective-permute-start | bytes 36872 | tf_op jit(solution)/shard_map/ppermute | solution.py:17
  118.3 2.3 %fusion = bf16[180,2048]{1,0:T(8,128)(2,1)S(1)} fusion(f32[180,2048]{1,0:T(8,128)} %select_n.201, bf16[180,512]{1,0:T(8,128)(2,1)} %reshape.949, bf16[2048,512]{1,0:T(8,128)(2,1)S(1)} %copy-done), kind=kOutput, calls=%fused_computation.2 | convolution fusion | flops 378224640 | bytes 4493312 | tf_op jit(solution)/shard_map/dot_general | solution.py:147
  121.8 3.8 %collective-permute-start.2 = (bf16[3,12,512]{2,0,1:T(4,128)(2,1)S(1)}, bf16[3,12,512]{2,0,1:T(4,128)(2,1)S(1)}, u32[]{:S(2)}, u32[]{:S(2)}) collective-permute-start(bf16[3,12,512]{2,0,1:T(4,128)(2,1)S(1)} %copy.48), channel_id=1, source_target_pairs={{0,1},{1,2},{2,3},{3,4},{4,5},{5,6},{6,7},{7,8},{8,9},{9,10},{10,1... | collective-permute-start | bytes 110600 | tf_op jit(solution)/shard_map/ppermute | solution.py:14
  125.9 1.3 copy.62
  127.4 1.3 copy.63
  (204 shorter events, 32.0 us)
Async XLA Ops:
  7.2 91.0 %all-gather.5.cloned.1.call-start = ((), (), s32[]{:S(2)}) async-start(), calls=%async_computation.1 | async-start | bytes 2228224 | tf_op jit(solution)/shard_map/all_gather | solution.py:76
  7.9 102.4 %all-gather.3.cloned.1.call-start = ((), (), s32[]{:S(2)}) async-start(), calls=%async_computation | async-start | bytes 2228224 | tf_op jit(solution)/shard_map/all_gather | solution.py:77
  9.5 36.9 %copy-start.41 = (bf16[32,512]{1,0:T(8,128)(2,1)S(1)}, bf16[32,512]{1,0:T(8,128)(2,1)}, u32[]{:S(2)}) copy-start(bf16[32,512]{1,0:T(8,128)(2,1)} %param.15) | copy-start | bytes 98308
  33.0 35.1 %copy-start.55 = (f32[7,512]{1,0:T(8,128)S(1)}, f32[7,512]{1,0:T(8,128)}, u32[]{:S(2)}) copy-start(f32[7,512]{1,0:T(8,128)} %param.17) | copy-start | bytes 43012
  33.0 35.1 %copy-start.54 = (f32[3,3,512]{2,1,0:T(4,128)S(1)}, f32[3,3,512]{2,1,0:T(4,128)}, u32[]{:S(2)}) copy-start(f32[3,3,512]{2,1,0:T(4,128)} %param.16) | copy-start | bytes 55300
  33.3 31.3 %copy-start.15 = (bf16[180,512]{1,0:T(8,128)(2,1)}, bf16[180,512]{1,0:T(8,128)(2,1)S(1)}, u32[]{:S(2)}) copy-start(bf16[180,512]{1,0:T(8,128)(2,1)S(1)} %convolution_convert_fusion.2) | copy-start | bytes 552964
  34.0 55.3 %collective-permute-start.8 = (bf16[1,12,512]{2,1,0:T(8,128)(2,1)}, bf16[1,12,512]{2,1,0:T(8,128)(2,1)}, u32[]{:S(2)}, u32[]{:S(2)}) collective-permute-start(bf16[1,12,512]{2,1,0:T(8,128)(2,1)} %get-tuple-element.18), channel_id=1, source_target_pairs={{0,1},{1,2},{2,3},{3,4},{4,5},{5,6},{6,7},{7,8},{8,9},{9,10},{10,1... | collective-permute-start | bytes 36872 | tf_op jit(solution)/shard_map/ppermute | solution.py:14
  37.7 55.1 %collective-permute-start.9 = (bf16[1,12,512]{2,1,0:T(8,128)(2,1)}, bf16[1,12,512]{2,1,0:T(8,128)(2,1)}, u32[]{:S(2)}, u32[]{:S(2)}) collective-permute-start(bf16[1,12,512]{2,1,0:T(8,128)(2,1)} %get-tuple-element.19), channel_id=1, source_target_pairs={{1,0},{2,1},{3,2},{4,3},{5,4},{6,5},{7,6},{8,7},{9,8},{10,9},{11,1... | collective-permute-start | bytes 36872 | tf_op jit(solution)/shard_map/ppermute | solution.py:17
  40.3 54.0 %collective-permute-start.7 = (bf16[1,12,512]{2,0,1:T(2,128)(2,1)}, bf16[1,12,512]{2,0,1:T(2,128)(2,1)}, u32[]{:S(2)}, u32[]{:S(2)}) collective-permute-start(bf16[1,12,512]{2,0,1:T(2,128)(2,1)} %copy.57), channel_id=1, source_target_pairs={{1,0},{2,1},{3,2},{4,3},{5,4},{6,5},{7,6},{8,7},{9,8},{10,9},{11,1... | collective-permute-start | bytes 36872 | tf_op jit(solution)/shard_map/ppermute | solution.py:17
  42.8 51.5 %collective-permute-start.6 = (bf16[1,12,512]{2,0,1:T(2,128)(2,1)}, bf16[1,12,512]{2,0,1:T(2,128)(2,1)}, u32[]{:S(2)}, u32[]{:S(2)}) collective-permute-start(bf16[1,12,512]{2,0,1:T(2,128)(2,1)} %copy.56), channel_id=1, source_target_pairs={{0,1},{1,2},{2,3},{3,4},{4,5},{5,6},{6,7},{7,8},{8,9},{9,10},{10,1... | collective-permute-start | bytes 36872 | tf_op jit(solution)/shard_map/ppermute | solution.py:14
  64.3 7.1 %copy-start.5 = (bf16[15,12,2048]{2,0,1:T(8,128)(2,1)S(1)}, bf16[15,12,2048]{2,0,1:T(8,128)(2,1)}, u32[]{:S(2)}) copy-start(bf16[15,12,2048]{2,0,1:T(8,128)(2,1)} %param.9) | copy-start | bytes 2211844
  65.9 29.7 %collective-permute-start.5 = (bf16[3,12,512]{2,0,1:T(4,128)(2,1)}, bf16[3,12,512]{2,0,1:T(4,128)(2,1)}, u32[]{:S(2)}, u32[]{:S(2)}) collective-permute-start(bf16[3,12,512]{2,0,1:T(4,128)(2,1)} %copy.54), channel_id=1, source_target_pairs={{1,0},{2,1},{3,2},{4,3},{5,4},{6,5},{7,6},{8,7},{9,8},{10,9},{11,1... | collective-permute-start | bytes 110600 | tf_op jit(solution)/shard_map/ppermute | solution.py:17
  68.1 28.5 %copy-start.56 = (f32[1,512]{1,0:T(1,128)}, f32[1,512]{1,0:T(1,128)S(1)}, u32[]{:S(2)}) copy-start(f32[1,512]{1,0:T(1,128)S(1)} %get-tuple-element.37) | copy-start | bytes 6148
  68.2 25.5 %copy-start.48 = (f32[1,1,512]{2,1,0:T(1,128)}, f32[1,1,512]{2,1,0:T(1,128)S(1)}, u32[]{:S(2)}) copy-start(f32[1,1,512]{2,1,0:T(1,128)S(1)} %get-tuple-element.28) | copy-start | bytes 6148
  68.2 25.5 %copy-start.50 = (f32[1,1,512]{2,1,0:T(1,128)}, f32[1,1,512]{2,1,0:T(1,128)S(1)}, u32[]{:S(2)}) copy-start(f32[1,1,512]{2,1,0:T(1,128)S(1)} %get-tuple-element.29) | copy-start | bytes 6148
  68.2 25.5 %copy-start.52 = (f32[1,1,512]{2,1,0:T(1,128)}, f32[1,1,512]{2,1,0:T(1,128)S(1)}, u32[]{:S(2)}) copy-start(f32[1,1,512]{2,1,0:T(1,128)S(1)} %get-tuple-element.30) | copy-start | bytes 6148
  87.9 5.8 %copy-start.11 = (f32[15,12,512]{2,1,0:T(8,128)S(1)}, f32[15,12,512]{2,1,0:T(8,128)}, u32[]{:S(2)}) copy-start(f32[15,12,512]{2,1,0:T(8,128)} %reshape.954) | copy-start | bytes 1105924
  89.3 6.3 %collective-permute-start.4 = (bf16[3,12,512]{2,0,1:T(4,128)(2,1)S(1)}, bf16[3,12,512]{2,0,1:T(4,128)(2,1)S(1)}, u32[]{:S(2)}, u32[]{:S(2)}) collective-permute-start(bf16[3,12,512]{2,0,1:T(4,128)(2,1)S(1)} %copy-done.39), channel_id=1, source_target_pairs={{0,1},{1,2},{2,3},{3,4},{4,5},{5,6},{6,7},{7,8},{8,9},{9,10},{10,1... | collective-permute-start | bytes 110600 | tf_op jit(solution)/shard_map/ppermute | solution.py:14
  98.1 12.2 %copy-start.7 = (bf16[180,2048]{1,0:T(8,128)(2,1)S(1)}, bf16[180,2048]{1,0:T(8,128)(2,1)}, u32[]{:S(2)}) copy-start(bf16[180,2048]{1,0:T(8,128)(2,1)} %max.13) | copy-start | bytes 2211844
  100.5 17.8 %copy-start = (bf16[2048,512]{1,0:T(8,128)(2,1)S(1)}, bf16[2048,512]{1,0:T(8,128)(2,1)}, u32[]{:S(2)}) copy-start(bf16[2048,512]{1,0:T(8,128)(2,1)} %all-gather.5.cloned.1.call-done) | copy-start | bytes 6291460
  100.5 30.5 %collective-permute-start.3 = (bf16[3,12,512]{2,0,1:T(4,128)(2,1)S(1)}, bf16[3,12,512]{2,0,1:T(4,128)(2,1)S(1)}, u32[]{:S(2)}, u32[]{:S(2)}) collective-permute-start(bf16[3,12,512]{2,0,1:T(4,128)(2,1)S(1)} %copy.49), channel_id=1, source_target_pairs={{1,0},{2,1},{3,2},{4,3},{5,4},{6,5},{7,6},{8,7},{9,8},{10,9},{11,1... | collective-permute-start | bytes 110600 | tf_op jit(solution)/shard_map/ppermute | solution.py:17
  113.1 15.6 %collective-permute-start = (bf16[1,12,512]{2,1,0:T(8,128)(2,1)}, bf16[1,12,512]{2,1,0:T(8,128)(2,1)}, u32[]{:S(2)}, u32[]{:S(2)}) collective-permute-start(bf16[1,12,512]{2,1,0:T(8,128)(2,1)} %get-tuple-element.22), channel_id=1, source_target_pairs={{0,1},{1,2},{2,3},{3,4},{4,5},{5,6},{6,7},{7,8},{8,9},{9,10},{10,1... | collective-permute-start | bytes 36872 | tf_op jit(solution)/shard_map/ppermute | solution.py:14
  116.0 12.6 %collective-permute-start.1 = (bf16[1,12,512]{2,1,0:T(8,128)(2,1)}, bf16[1,12,512]{2,1,0:T(8,128)(2,1)}, u32[]{:S(2)}, u32[]{:S(2)}) collective-permute-start(bf16[1,12,512]{2,1,0:T(8,128)(2,1)} %get-tuple-element.23), channel_id=1, source_target_pairs={{1,0},{2,1},{3,2},{4,3},{5,4},{6,5},{7,6},{8,7},{9,8},{10,9},{11,1... | collective-permute-start | bytes 36872 | tf_op jit(solution)/shard_map/ppermute | solution.py:17
  121.8 9.2 %collective-permute-start.2 = (bf16[3,12,512]{2,0,1:T(4,128)(2,1)S(1)}, bf16[3,12,512]{2,0,1:T(4,128)(2,1)S(1)}, u32[]{:S(2)}, u32[]{:S(2)}) collective-permute-start(bf16[3,12,512]{2,0,1:T(4,128)(2,1)S(1)} %copy.48), channel_id=1, source_target_pairs={{0,1},{1,2},{2,3},{3,4},{4,5},{5,6},{6,7},{7,8},{8,9},{9,10},{10,1... | collective-permute-start | bytes 110600 | tf_op jit(solution)/shard_map/ppermute | solution.py:14
  (50 other events, 121.3 us)
Sparse Core Ops, SparseCore 0:
  10.1 47.4 all-gather.4
  68.1 42.1 all-gather.2
where the time goes:
time: 142 us; the launch traced here: 141 us
  blocking collectives  39.5 us (28%)
  local copies, waits for them, and re-layouts  28.5 us (20%)
  starting transfers between devices  27.8 us (20%)
  between operations  15.2 us (11%)
  other arithmetic  12.5 us (9%)
  matrix products  8.93 us (6%)
  waiting for transfers between devices  8.54 us (6%)
    all_gather x1, blocking collectives, local(): lax.all_gather(square_point, 'rows', axis=0, tiled=True)  22.4 us
    ppermute x5, starting transfers between devices, with_halo(): lax.ppermute(lax.slice_in_dim(block, block.shape[dim] - width, None, axis...  17.5 us
    all_gather x1, blocking collectives, local(): lax.all_gather(column_point, 'rows', axis=0, tiled=True)  17.1 us
    ppermute x5, starting transfers between devices, with_halo(): lax.ppermute(lax.slice_in_dim(block, 0, width, axis=dim), axis, backward)  10.2 us
    unnamed x127, local copies, waits for them, and re-layouts  8.35 us
    all_gather x1, waiting for transfers between devices, local(): lax.all_gather(newer_weight, 'rows', axis=0, tiled=True)  7.82 us
    select_n x2, local copies, waits for them, and re-layouts, local(): older_mask = jnp.where(older_flat > 0, 1.0, 0.0).astype(jnp.float32)  3.64 us
    slice x10, local copies, waits for them, and re-layouts, with_halo(): lax.slice_in_dim(block, block.shape[dim] - width, None, axis=dim)  3.23 us
  transfers between devices with their start and end apart: 12, of which 1 were waited for; matrix products, arithmetic and copies ran while one was open for 31% of the time, Pallas kernels for 0%

commit v1 on v0

--- a/solution.py
+++ b/solution.py
@@ -81,7 +81,9 @@
     older_mixed = older_sum.astype(jnp.bfloat16).reshape(shape_three)
     newer_mixed = newer_sum.astype(jnp.bfloat16).reshape(shape_three)
     square_full, column_full = (
-        lax.all_gather(square_point, "rows", axis=0, tiled=True),
+        jnp.concatenate(
+            lax.all_to_all(jnp.stack([square_point] * lax.axis_size("rows")), "rows", 0, 0), axis=0
+        ),
         lax.all_gather(column_point, "rows", axis=0, tiled=True),
     )
     older_rim = with_halo(older_mixed, (("rows", 0),), 3)

time: 142 us -> 136 us (0.958)
  blocking collectives: 39.5 us -> 23 us
  starting transfers between devices: 27.8 us -> 37.8 us
  local copies, waits for them, and re-layouts: 28.5 us -> 23.2 us
  waiting for transfers between devices: 8.54 us -> 13.1 us
  matrix products: 8.93 us -> 11 us
    all_gather x1 -> x0, blocking collectives: 22.4 us -> none  [local(): lax.all_gather(square_point, 'rows', axis=0, tiled=True)]
    all_to_all x0 -> x1, starting transfers between devices: none -> 10.8 us  [local(): lax.all_to_all(jnp.stack([square_point] * lax.axis_size('rows')), 'rows',...]
    all_gather x1, blocking collectives: 17.1 us -> 23 us  [local(): lax.all_gather(column_point, 'rows', axis=0, tiled=True)]
    all_gather x1, waiting for transfers between devices: 7.82 us -> 10.3 us  [local(): lax.all_gather(newer_weight, 'rows', axis=0, tiled=True)]
    unnamed x127 -> x119, local copies, waits for them, and re-layouts: 8.35 us -> 5.9 us
    ppermute x5, waiting for transfers between devices: 0.01 us -> 2.12 us  [with_halo(): lax.ppermute(lax.slice_in_dim(block, 0, width, axis=dim), axis, backward)]
    ppermute x5, starting transfers between devices: 17.5 us -> 15.9 us  [with_halo(): lax.ppermute(lax.slice_in_dim(block, block.shape[dim] - width, None, axis...]
    another operation x0 -> x1, local copies, waits for them, and re-layouts: none -> 1.61 us  [local(): jnp.stack([square_point] * lax.axis_size('rows'))]
  transfers between devices with their start and end apart: 12 -> 13, of which waited for: 1 -> 2; matrix products, arithmetic and copies ran while one was open for 31% -> 30% of each run, Pallas kernels for 0% -> 0%
where the time goes in v1:
time: 136 us; the launch traced here: 135 us
  starting transfers between devices  37.8 us (28%)
  local copies, waits for them, and re-layouts  23.2 us (17%)
  blocking collectives  23 us (17%)
  between operations  15.2 us (11%)
  waiting for transfers between devices  13.1 us (10%)
  other arithmetic  11.7 us (9%)
  matrix products  11 us (8%)
    all_gather x1, blocking collectives, local(): lax.all_gather(column_point, 'rows', axis=0, tiled=True)  23 us
    ppermute x5, starting transfers between devices, with_halo(): lax.ppermute(lax.slice_in_dim(block, block.shape[dim] - width, None, axis...  15.9 us
    ppermute x5, starting transfers between devices, with_halo(): lax.ppermute(lax.slice_in_dim(block, 0, width, axis=dim), axis, backward)  11 us
    all_to_all x1, starting transfers between devices, local(): lax.all_to_all(jnp.stack([square_point] * lax.axis_size('rows')), 'rows',...  10.8 us
    all_gather x1, waiting for transfers between devices, local(): lax.all_gather(newer_weight, 'rows', axis=0, tiled=True)  10.3 us
    unnamed x119, local copies, waits for them, and re-layouts  5.9 us
  transfers between devices with their start and end apart: 13, of which 2 were waited for; matrix products, arithmetic and copies ran while one was open for 30% of the time, Pallas kernels for 0%

profile of v1, /device:TPU:1, one launch (start us, length us, event | category | flops | bytes accessed | tf_op | source)
XLA Modules:
  0.0 135.0 jit_solution(3497305045421964107)
XLA Ops:
  7.9 1.6 %stack.2 = bf16[16,32,512]{2,1,0:T(8,128)(2,1)} broadcast(bf16[32,512]{1,0:T(8,128)(2,1)} %param.14), dimensions={1,2} | broadcast | bytes 557056 | tf_op jit(solution)/shard_map/stack | solution.py:85
  9.5 10.8 %all-to-all-start = ((bf16[16,32,512]{2,1,0:T(8,128)(2,1)}), bf16[16,32,512]{2,1,0:T(8,128)(2,1)}, u32[]{:S(2)}, u32[]{:S(2)}) async-start(bf16[16,32,512]{2,1,0:T(8,128)(2,1)} %stack.2), calls=%async_computation | async-start | bytes 1048576 | tf_op jit(solution)/shard_map/all_to_all | solution.py:85
  21.7 2.3 %collective-permute-start.7 = (bf16[1,12,512]{2,0,1:T(2,128)(2,1)}, bf16[1,12,512]{2,0,1:T(2,128)(2,1)}, u32[]{:S(2)}, u32[]{:S(2)}) collective-permute-start(bf16[1,12,512]{2,0,1:T(2,128)(2,1)} %copy.57), channel_id=1, source_target_pairs={{1,0},{2,1},{3,2},{4,3},{5,4},{6,5},{7,6},{8,7},{9,8},{10,9},{11,1... | collective-permute-start | bytes 36872 | tf_op jit(solution)/shard_map/ppermute | solution.py:17
  24.7 3.5 %collective-permute-start.6 = (bf16[1,12,512]{2,0,1:T(2,128)(2,1)}, bf16[1,12,512]{2,0,1:T(2,128)(2,1)}, u32[]{:S(2)}, u32[]{:S(2)}) collective-permute-start(bf16[1,12,512]{2,0,1:T(2,128)(2,1)} %copy.56), channel_id=1, source_target_pairs={{0,1},{1,2},{2,3},{3,4},{4,5},{5,6},{6,7},{7,8},{8,9},{9,10},{10,1... | collective-permute-start | bytes 36872 | tf_op jit(solution)/shard_map/ppermute | solution.py:14
  28.2 23.0 %all_gather.11 = bf16[512,512]{1,0:T(8,128)(2,1)S(1)} all-gather(bf16[32,512]{1,0:T(8,128)(2,1)S(1)} %copy-done.37), channel_id=1, replica_groups=mesh['dp'=32,'rows'=16] {'rows'}, dimensions={0}, use_global_device_ids=true | all-gather | bytes 557056 | tf_op jit(solution)/shard_map/all_gather | solution.py:87
  53.0 2.1 %collective-permute-start.5 = (bf16[3,12,512]{2,0,1:T(4,128)(2,1)}, bf16[3,12,512]{2,0,1:T(4,128)(2,1)}, u32[]{:S(2)}, u32[]{:S(2)}) collective-permute-start(bf16[3,12,512]{2,0,1:T(4,128)(2,1)} %copy.54), channel_id=1, source_target_pairs={{1,0},{2,1},{3,2},{4,3},{5,4},{6,5},{7,6},{8,7},{9,8},{10,9},{11,1... | collective-permute-start | bytes 110600 | tf_op jit(solution)/shard_map/ppermute | solution.py:17
  55.7 3.5 %collective-permute-start.4 = (bf16[3,12,512]{2,0,1:T(4,128)(2,1)}, bf16[3,12,512]{2,0,1:T(4,128)(2,1)}, u32[]{:S(2)}, u32[]{:S(2)}) collective-permute-start(bf16[3,12,512]{2,0,1:T(4,128)(2,1)} %copy.53), channel_id=1, source_target_pairs={{0,1},{1,2},{2,3},{3,4},{4,5},{5,6},{6,7},{7,8},{8,9},{9,10},{10,1... | collective-permute-start | bytes 110600 | tf_op jit(solution)/shard_map/ppermute | solution.py:14
  63.7 1.3 compare_select_fusion
  72.9 1.4 %select_n.201 = f32[180,2048]{1,0:T(8,128)} reshape(f32[15,12,2048]{2,1,0:T(8,128)S(1)} %copy.60) | data formatting | bytes 2949120 | tf_op jit(solution)/shard_map/jit(_where)/select_n | solution.py:147
  75.7 1.3 select_n.203
  79.0 1.5 %convolution_convert_fusion.2 = bf16[180,512]{1,0:T(8,128)(2,1)S(1)} fusion(bf16[512,512]{1,0:T(8,128)(2,1)} %bitcast.11, bf16[180,2048]{1,0:T(8,128)(2,1)} %copy-done.4), kind=kOutput, calls=%fused_computation.8 | convolution fusion | flops 94464000 | bytes 897024 | tf_op jit(solution)/shard_map/dot_general | solution.py:120
  80.5 1.9 %collective-permute-start.8 = (bf16[1,12,512]{2,1,0:T(8,128)(2,1)S(1)}, bf16[1,12,512]{2,1,0:T(8,128)(2,1)S(1)}, u32[]{:S(2)}, u32[]{:S(2)}) collective-permute-start(bf16[1,12,512]{2,1,0:T(8,128)(2,1)S(1)} %get-tuple-element.18), channel_id=1, source_target_pairs={{0,1},{1,2},{2,3},{3,4},{4,5},{5,6},{6,7},{7,8},{8,9},{9,10},{10,1... | collective-permute-start | bytes 36872 | tf_op jit(solution)/shard_map/ppermute | solution.py:14
  82.4 2.4 %collective-permute-start.9 = (bf16[1,12,512]{2,1,0:T(8,128)(2,1)S(1)}, bf16[1,12,512]{2,1,0:T(8,128)(2,1)S(1)}, u32[]{:S(2)}, u32[]{:S(2)}) collective-permute-start(bf16[1,12,512]{2,1,0:T(8,128)(2,1)S(1)} %get-tuple-element.19), channel_id=1, source_target_pairs={{1,0},{2,1},{3,2},{4,3},{5,4},{6,5},{7,6},{8,7},{9,8},{10,9},{11,1... | collective-permute-start | bytes 36872 | tf_op jit(solution)/shard_map/ppermute | solution.py:17
  85.8 2.1 %collective-permute-done.9 = bf16[1,12,512]{2,1,0:T(8,128)(2,1)S(1)} collective-permute-done((bf16[1,12,512]{2,1,0:T(8,128)(2,1)S(1)}, bf16[1,12,512]{2,1,0:T(8,128)(2,1)S(1)}, u32[]{:S(2)}, u32[]{:S(2)}) %collective-permute-start.9) | collective-permute-done | bytes 12320 | tf_op jit(solution)/shard_map/ppermute | solution.py:17
  89.2 2.2 %convolution_convert_fusion.4 = bf16[180,512]{1,0:T(8,128)(2,1)S(1)} fusion(bf16[180,2048]{1,0:T(8,128)(2,1)S(1)} %copy-done.9, bf16[2048,512]{1,0:T(8,128)(2,1)} %all-gather.5.cloned.1.call-done), kind=kOutput, calls=%fused_computation.10 | convolution fusion | flops 377579520 | bytes 3018752 | tf_op jit(solution)/shard_map/dot_general | solution.py:79
  91.5 2.1 %collective-permute-start.3 = (bf16[3,12,512]{2,0,1:T(4,128)(2,1)S(1)}, bf16[3,12,512]{2,0,1:T(4,128)(2,1)S(1)}, u32[]{:S(2)}, u32[]{:S(2)}) collective-permute-start(bf16[3,12,512]{2,0,1:T(4,128)(2,1)S(1)} %copy.49), channel_id=1, source_target_pairs={{1,0},{2,1},{3,2},{4,3},{5,4},{6,5},{7,6},{8,7},{9,8},{10,9},{11,1... | collective-permute-start | bytes 110600 | tf_op jit(solution)/shard_map/ppermute | solution.py:17
  93.6 10.3 %all-gather.3.cloned.1.call-done = bf16[2048,512]{1,0:T(8,128)(2,1)} async-done(((bf16[128,512]{1,0:T(8,128)(2,1)}), bf16[2048,512]{1,0:T(8,128)(2,1)}) %all-gather.3.cloned.1.call-update) | async-done | bytes 2097168 | tf_op jit(solution)/shard_map/all_gather | solution.py:77
  103.9 2.1 %convolution_convert_fusion.5 = bf16[180,512]{1,0:T(8,128)(2,1)S(1)} fusion(bf16[180,2048]{1,0:T(8,128)(2,1)S(1)} %copy-done.8, bf16[2048,512]{1,0:T(8,128)(2,1)} %all-gather.3.cloned.1.call-done), kind=kOutput, calls=%fused_computation.11 | convolution fusion | flops 377579520 | bytes 3018752 | tf_op jit(solution)/shard_map/dot_general | solution.py:80
  106.6 3.2 %collective-permute-start = (bf16[1,12,512]{2,1,0:T(8,128)(2,1)}, bf16[1,12,512]{2,1,0:T(8,128)(2,1)}, u32[]{:S(2)}, u32[]{:S(2)}) collective-permute-start(bf16[1,12,512]{2,1,0:T(8,128)(2,1)} %get-tuple-element.22), channel_id=1, source_target_pairs={{0,1},{1,2},{2,3},{3,4},{4,5},{5,6},{6,7},{7,8},{8,9},{9,10},{10,1... | collective-permute-start | bytes 36872 | tf_op jit(solution)/shard_map/ppermute | solution.py:14
  109.8 2.2 %collective-permute-start.1 = (bf16[1,12,512]{2,1,0:T(8,128)(2,1)}, bf16[1,12,512]{2,1,0:T(8,128)(2,1)}, u32[]{:S(2)}, u32[]{:S(2)}) collective-permute-start(bf16[1,12,512]{2,1,0:T(8,128)(2,1)} %get-tuple-element.23), channel_id=1, source_target_pairs={{1,0},{2,1},{3,2},{4,3},{5,4},{6,5},{7,6},{8,7},{9,8},{10,9},{11,1... | collective-permute-start | bytes 36872 | tf_op jit(solution)/shard_map/ppermute | solution.py:17
  112.0 2.2 %fusion = bf16[180,2048]{1,0:T(8,128)(2,1)S(1)} fusion(f32[180,2048]{1,0:T(8,128)} %select_n.201, bf16[180,512]{1,0:T(8,128)(2,1)S(1)} %reshape.955, bf16[2048,512]{1,0:T(8,128)(2,1)S(1)} %copy-done), kind=kOutput, calls=%fused_computation.2 | convolution fusion | flops 378224640 | bytes 4493312 | tf_op jit(solution)/shard_map/dot_general | solution.py:149
  115.4 3.8 %collective-permute-start.2 = (bf16[3,12,512]{2,0,1:T(4,128)(2,1)S(1)}, bf16[3,12,512]{2,0,1:T(4,128)(2,1)S(1)}, u32[]{:S(2)}, u32[]{:S(2)}) collective-permute-start(bf16[3,12,512]{2,0,1:T(4,128)(2,1)S(1)} %copy.48), channel_id=1, source_target_pairs={{0,1},{1,2},{2,3},{3,4},{4,5},{5,6},{6,7},{7,8},{8,9},{9,10},{10,1... | collective-permute-start | bytes 110600 | tf_op jit(solution)/shard_map/ppermute | solution.py:14
  119.5 1.3 copy.62
  123.7 1.3 convolution_convert_fusion.1
  (198 shorter events, 30.5 us)
Async XLA Ops:
  7.2 13.2 %copy-start.15 = (bf16[15,12,2048]{2,0,1:T(8,128)(2,1)S(1)}, bf16[15,12,2048]{2,0,1:T(8,128)(2,1)}, u32[]{:S(2)}) copy-start(bf16[15,12,2048]{2,0,1:T(8,128)(2,1)} %param.11) | copy-start | bytes 2211844
  7.2 82.1 %all-gather.5.cloned.1.call-start = ((), (), s32[]{:S(2)}) async-start(), calls=%async_computation.2 | async-start | bytes 2228224 | tf_op jit(solution)/shard_map/all_gather | solution.py:76
  9.5 69.4 %all-to-all-start = ((bf16[16,32,512]{2,1,0:T(8,128)(2,1)}), bf16[16,32,512]{2,1,0:T(8,128)(2,1)}, u32[]{:S(2)}, u32[]{:S(2)}) async-start(bf16[16,32,512]{2,1,0:T(8,128)(2,1)} %stack.2), calls=%async_computation | async-start | bytes 1048576 | tf_op jit(solution)/shard_map/all_to_all | solution.py:85
  20.3 83.5 %all-gather.3.cloned.1.call-start = ((), (), s32[]{:S(2)}) async-start(), calls=%async_computation.1 | async-start | bytes 2228224 | tf_op jit(solution)/shard_map/all_gather | solution.py:77
  21.0 39.1 %copy-start.4 = (bf16[180,2048]{1,0:T(8,128)(2,1)}, bf16[180,2048]{1,0:T(8,128)(2,1)S(1)}, u32[]{:S(2)}) copy-start(bf16[180,2048]{1,0:T(8,128)(2,1)S(1)} %reshape.952) | copy-start | bytes 2211844
  21.7 38.4 %copy-start.51 = (f32[7,512]{1,0:T(8,128)S(1)}, f32[7,512]{1,0:T(8,128)}, u32[]{:S(2)}) copy-start(f32[7,512]{1,0:T(8,128)} %param.17) | copy-start | bytes 43012
  21.7 55.4 %collective-permute-start.7 = (bf16[1,12,512]{2,0,1:T(2,128)(2,1)}, bf16[1,12,512]{2,0,1:T(2,128)(2,1)}, u32[]{:S(2)}, u32[]{:S(2)}) collective-permute-start(bf16[1,12,512]{2,0,1:T(2,128)(2,1)} %copy.57), channel_id=1, source_target_pairs={{1,0},{2,1},{3,2},{4,3},{5,4},{6,5},{7,6},{8,7},{9,8},{10,9},{11,1... | collective-permute-start | bytes 36872 | tf_op jit(solution)/shard_map/ppermute | solution.py:17
  24.0 36.1 %copy-start.50 = (f32[3,3,512]{2,1,0:T(4,128)S(1)}, f32[3,3,512]{2,1,0:T(4,128)}, u32[]{:S(2)}) copy-start(f32[3,3,512]{2,1,0:T(4,128)} %param.16) | copy-start | bytes 55300
  24.7 35.5 %copy-start.6 = (bf16[15,12,2048]{2,0,1:T(8,128)(2,1)S(1)}, bf16[15,12,2048]{2,0,1:T(8,128)(2,1)}, u32[]{:S(2)}) copy-start(bf16[15,12,2048]{2,0,1:T(8,128)(2,1)} %param.9) | copy-start | bytes 2211844
  24.7 52.4 %collective-permute-start.6 = (bf16[1,12,512]{2,0,1:T(2,128)(2,1)}, bf16[1,12,512]{2,0,1:T(2,128)(2,1)}, u32[]{:S(2)}, u32[]{:S(2)}) collective-permute-start(bf16[1,12,512]{2,0,1:T(2,128)(2,1)} %copy.56), channel_id=1, source_target_pairs={{0,1},{1,2},{2,3},{3,4},{4,5},{5,6},{6,7},{7,8},{8,9},{9,10},{10,1... | collective-permute-start | bytes 36872 | tf_op jit(solution)/shard_map/ppermute | solution.py:14
  53.0 25.0 %collective-permute-start.5 = (bf16[3,12,512]{2,0,1:T(4,128)(2,1)}, bf16[3,12,512]{2,0,1:T(4,128)(2,1)}, u32[]{:S(2)}, u32[]{:S(2)}) collective-permute-start(bf16[3,12,512]{2,0,1:T(4,128)(2,1)} %copy.54), channel_id=1, source_target_pairs={{1,0},{2,1},{3,2},{4,3},{5,4},{6,5},{7,6},{8,7},{9,8},{10,9},{11,1... | collective-permute-start | bytes 110600 | tf_op jit(solution)/shard_map/ppermute | solution.py:17
  55.7 22.3 %collective-permute-start.4 = (bf16[3,12,512]{2,0,1:T(4,128)(2,1)}, bf16[3,12,512]{2,0,1:T(4,128)(2,1)}, u32[]{:S(2)}, u32[]{:S(2)}) collective-permute-start(bf16[3,12,512]{2,0,1:T(4,128)(2,1)} %copy.53), channel_id=1, source_target_pairs={{0,1},{1,2},{2,3},{3,4},{4,5},{5,6},{6,7},{7,8},{8,9},{9,10},{10,1... | collective-permute-start | bytes 110600 | tf_op jit(solution)/shard_map/ppermute | solution.py:14
  60.1 24.7 %copy-start.52 = (f32[1,512]{1,0:T(1,128)}, f32[1,512]{1,0:T(1,128)S(1)}, u32[]{:S(2)}) copy-start(f32[1,512]{1,0:T(1,128)S(1)} %get-tuple-element.37) | copy-start | bytes 6148
  60.1 27.8 %copy-start.44 = (f32[1,1,512]{2,1,0:T(1,128)}, f32[1,1,512]{2,1,0:T(1,128)S(1)}, u32[]{:S(2)}) copy-start(f32[1,1,512]{2,1,0:T(1,128)S(1)} %get-tuple-element.28) | copy-start | bytes 6148
  60.2 27.8 %copy-start.46 = (f32[1,1,512]{2,1,0:T(1,128)}, f32[1,1,512]{2,1,0:T(1,128)S(1)}, u32[]{:S(2)}) copy-start(f32[1,1,512]{2,1,0:T(1,128)S(1)} %get-tuple-element.29) | copy-start | bytes 6148
  60.2 27.8 %copy-start.48 = (f32[1,1,512]{2,1,0:T(1,128)}, f32[1,1,512]{2,1,0:T(1,128)S(1)}, u32[]{:S(2)}) copy-start(f32[1,1,512]{2,1,0:T(1,128)S(1)} %get-tuple-element.30) | copy-start | bytes 6148
  80.5 5.3 %collective-permute-start.8 = (bf16[1,12,512]{2,1,0:T(8,128)(2,1)S(1)}, bf16[1,12,512]{2,1,0:T(8,128)(2,1)S(1)}, u32[]{:S(2)}, u32[]{:S(2)}) collective-permute-start(bf16[1,12,512]{2,1,0:T(8,128)(2,1)S(1)} %get-tuple-element.18), channel_id=1, source_target_pairs={{0,1},{1,2},{2,3},{3,4},{4,5},{5,6},{6,7},{7,8},{8,9},{9,10},{10,1... | collective-permute-start | bytes 36872 | tf_op jit(solution)/shard_map/ppermute | solution.py:14
  82.4 5.5 %collective-permute-start.9 = (bf16[1,12,512]{2,1,0:T(8,128)(2,1)S(1)}, bf16[1,12,512]{2,1,0:T(8,128)(2,1)S(1)}, u32[]{:S(2)}, u32[]{:S(2)}) collective-permute-start(bf16[1,12,512]{2,1,0:T(8,128)(2,1)S(1)} %get-tuple-element.19), channel_id=1, source_target_pairs={{1,0},{2,1},{3,2},{4,3},{5,4},{6,5},{7,6},{8,7},{9,8},{10,9},{11,1... | collective-permute-start | bytes 36872 | tf_op jit(solution)/shard_map/ppermute | solution.py:17
  89.2 14.6 %copy-start.8 = (bf16[180,2048]{1,0:T(8,128)(2,1)S(1)}, bf16[180,2048]{1,0:T(8,128)(2,1)}, u32[]{:S(2)}) copy-start(bf16[180,2048]{1,0:T(8,128)(2,1)} %max.13) | copy-start | bytes 2211844
  91.5 20.5 %copy-start = (bf16[2048,512]{1,0:T(8,128)(2,1)S(1)}, bf16[2048,512]{1,0:T(8,128)(2,1)}, u32[]{:S(2)}) copy-start(bf16[2048,512]{1,0:T(8,128)(2,1)} %all-gather.5.cloned.1.call-done) | copy-start | bytes 6291460
  91.5 33.5 %collective-permute-start.3 = (bf16[3,12,512]{2,0,1:T(4,128)(2,1)S(1)}, bf16[3,12,512]{2,0,1:T(4,128)(2,1)S(1)}, u32[]{:S(2)}, u32[]{:S(2)}) collective-permute-start(bf16[3,12,512]{2,0,1:T(4,128)(2,1)S(1)} %copy.49), channel_id=1, source_target_pairs={{1,0},{2,1},{3,2},{4,3},{5,4},{6,5},{7,6},{8,7},{9,8},{10,9},{11,1... | collective-permute-start | bytes 110600 | tf_op jit(solution)/shard_map/ppermute | solution.py:17
  106.6 15.7 %collective-permute-start = (bf16[1,12,512]{2,1,0:T(8,128)(2,1)}, bf16[1,12,512]{2,1,0:T(8,128)(2,1)}, u32[]{:S(2)}, u32[]{:S(2)}) collective-permute-start(bf16[1,12,512]{2,1,0:T(8,128)(2,1)} %get-tuple-element.22), channel_id=1, source_target_pairs={{0,1},{1,2},{2,3},{3,4},{4,5},{5,6},{6,7},{7,8},{8,9},{9,10},{10,1... | collective-permute-start | bytes 36872 | tf_op jit(solution)/shard_map/ppermute | solution.py:14
  109.8 12.5 %collective-permute-start.1 = (bf16[1,12,512]{2,1,0:T(8,128)(2,1)}, bf16[1,12,512]{2,1,0:T(8,128)(2,1)}, u32[]{:S(2)}, u32[]{:S(2)}) collective-permute-start(bf16[1,12,512]{2,1,0:T(8,128)(2,1)} %get-tuple-element.23), channel_id=1, source_target_pairs={{1,0},{2,1},{3,2},{4,3},{5,4},{6,5},{7,6},{8,7},{9,8},{10,9},{11,1... | collective-permute-start | bytes 36872 | tf_op jit(solution)/shard_map/ppermute | solution.py:17
  115.4 9.6 %collective-permute-start.2 = (bf16[3,12,512]{2,0,1:T(4,128)(2,1)S(1)}, bf16[3,12,512]{2,0,1:T(4,128)(2,1)S(1)}, u32[]{:S(2)}, u32[]{:S(2)}) collective-permute-start(bf16[3,12,512]{2,0,1:T(4,128)(2,1)S(1)} %copy.48), channel_id=1, source_target_pairs={{0,1},{1,2},{2,3},{3,4},{4,5},{5,6},{6,7},{7,8},{8,9},{9,10},{10,1... | collective-permute-start | bytes 110600 | tf_op jit(solution)/shard_map/ppermute | solution.py:14
  (47 other events, 145.8 us)
Sparse Core Ops, SparseCore 0:
  10.1 49.7 all-gather.4
  62.0 41.8 all-gather.2
